TPU v7x, 256 devices: a whole 4x4x8 slice. The times are simulated.
256 devices in a mesh: tc: 128 (over z, x, y), pr: 2 (over core).
Axes of the slice: x: 4, y: 4, z: 8, core: 2. Of those that a mesh axis runs over, the one named last changes fastest.
Arguments:
- pivot_rhs: float32 [128, 1536, 64], P('tc', None, 'pr'), may hold values from -6 to 6
- pivot_inverse: bfloat16 [128, 1536, 1536], P('tc'), as said below
- pivot_owner: int32 [3], replicated, may hold values from 0 to 127, as said below
- coupling_left: bfloat16 [128, 2, 1536, 200], P('tc'), may hold values from -0.15625 to 0.15625
- coupling_right: bfloat16 [128, 2, 1536, 200], P('tc'), may hold values from -0.4375 to 0.4375
- coupling_ranks: int32 [128, 2], P('tc'), may hold values from 100 to 200, as said below
- future_left: bfloat16 [256, 3, 200, 1536], P('tc', None, None, 'pr'), may hold values from -0.15625 to 0.15625
- future_right: bfloat16 [256, 3, 200, 1536], P('tc', None, None, 'pr'), may hold values from -0.4375 to 0.4375
- future_ranks: int32 [256, 3], P('tc'), may hold values from 100 to 200, as said below
- future_rhs: float32 [256, 64, 1536], P('tc', None, 'pr'), may hold values from -6 to 6
Outputs:
- solved: bfloat16 [3, 1536, 64], P(None, None, 'pr')
- future_out: float32 [256, 64, 1536], P('tc', None, 'pr')
Inputs may be any that keep to these rules, and one draw needn't show every extreme that they name: `pivot_owner`: the 3 entries are distinct; entry p names the slot, and so the index of tc, that holds pivot p's tiles. `coupling_ranks`: entry [s, j] is the rank of the tile from the pivot in slot s to the pivot j + 1 places later. In every draw a tile that the window uses has rank exactly 200. `future_ranks`: in every draw one of these tiles has rank exactly 200. `pivot_inverse`: each tile is lower triangular.
All inputs are finite; a program needn't handle non-finite values.
Results may differ from a plain program's by a relative error of at most 0.007.
Values may be sent and summed in bfloat16 or wider, within the bound.
A program may use at most 64 MiB of HBM per device.

v0:
```python
import jax
import jax.numpy as jnp
from jax import lax
from jax.sharding import Mesh
from jax.sharding import PartitionSpec as P

TC = ("tc_0", "tc_1", "tc_2")


def padded_to(lines, count):
    spare = -lines.shape[0] % count
    if not spare:
        return lines
    return jnp.concatenate([lines, jnp.zeros((spare, *lines.shape[1:]), lines.dtype)])


def sent_to_all(shard, axis):
    count = lax.axis_size(axis)
    return lax.all_to_all(
        jnp.broadcast_to(shard[None], (count, *shard.shape)), axis, 0, 0, tiled=True
    )


def in_order(pieces, dim):
    pieces = jnp.moveaxis(pieces, 0, dim)
    shape = pieces.shape
    return pieces.reshape(*shape[:dim], shape[dim] * shape[dim + 1], *shape[dim + 2 :])


def gathered_by_axis(shard, axes, dim):
    far, near = axes
    pieces = sent_to_all(sent_to_all(shard, far), near)
    return in_order(pieces.swapaxes(0, 1).reshape(-1, *shard.shape), dim)


def in_blocks(shard, dim, count):
    shape = shard.shape
    pieces = shard.reshape(*shape[:dim], count, shape[dim] // count, *shape[dim + 1 :])
    return jnp.moveaxis(pieces, dim, 0)


def sum_at_owner(shard, axis, dim):
    pieces = in_blocks(shard, dim, lax.axis_size(axis))
    arrived = lax.all_to_all(pieces, axis, split_axis=0, concat_axis=0, tiled=True)
    return arrived.sum(axis=0)


def summed_rows(shard, axes, dim):
    far, near = axes
    own = sum_at_owner(in_blocks(shard, dim, lax.axis_size(far)), near, dim + 1)
    return jnp.sum(lax.all_to_all(own, far, 0, 0, tiled=True), axis=0)


def nested_sum(shard, axes):
    lines = shard.reshape(-1, shard.shape[-1])
    padded = padded_to(lines, lax.axis_size(axes[0]) * lax.axis_size(axes[1]))
    whole = gathered_by_axis(summed_rows(padded, axes, 0), axes, 0)
    return lax.slice_in_dim(whole, 0, len(lines)).reshape(shard.shape)


def over_copies(shard, axis):
    return sent_to_all(shard, axis).sum(axis=0)


def apply_weights(products, right_part, ranks_part):
    rank_ids = lax.broadcasted_iota(jnp.int32, products.shape, 3)
    weights = jnp.where(rank_ids < ranks_part[:, :, None, None], products, 0.0).astype(jnp.bfloat16)
    return jnp.einsum("fsqr,fsrb->fqb", weights, right_part, preferred_element_type=jnp.float32)


def local(
    pivot_rhs,
    pivot_inverse,
    pivot_owner,
    coupling_left,
    coupling_right,
    coupling_ranks,
    future_left,
    future_right,
    future_ranks,
    future_rhs,
):
    tile_count = pivot_owner.shape[0]
    rank_width = coupling_left.shape[3]
    device_index = lax.axis_index(TC)
    owned_flags = pivot_owner == device_index
    holds_pivot = jnp.any(owned_flags)
    own_pivot = jnp.sum(jnp.where(owned_flags, jnp.arange(tile_count, dtype=jnp.int32), 0))
    pending = pivot_rhs[0]
    inverse_tile = pivot_inverse[0]
    rank_ids = lax.broadcasted_iota(jnp.int32, (rank_width, 1), 0)
    solved = [None] * tile_count
    future_acc = future_rhs
    for current in reversed(range(tile_count)):
        pivot_in = pending.astype(jnp.bfloat16)
        local_solution = lax.dot_general(
            inverse_tile, pivot_in, (((0,), (0,)), ((), ())), preferred_element_type=jnp.float32
        ).astype(jnp.bfloat16)
        is_root = device_index == pivot_owner[current]
        masked_block = jnp.where(is_root, local_solution.astype(jnp.float32), 0.0)
        solved_block = nested_sum(masked_block, (("tc_0", "tc_1"), "tc_2")).astype(jnp.bfloat16)
        solved[current] = solved_block
        if current > 0:
            distance = current - own_pivot - 1
            active = jnp.logical_and(holds_pivot, distance >= 0)
            slot_entry = jnp.clip(distance, 0, tile_count - 2)
            left_tile = lax.dynamic_index_in_dim(coupling_left[0], slot_entry, 0, keepdims=False)
            right_tile = lax.dynamic_index_in_dim(coupling_right[0], slot_entry, 0, keepdims=False)
            rank_limit = lax.dynamic_index_in_dim(coupling_ranks[0], slot_entry, 0, keepdims=False)
            factor = lax.dot_general(
                left_tile,
                solved_block,
                (((0,), (0,)), ((), ())),
                preferred_element_type=jnp.float32,
            )
            factor = jnp.where(rank_ids < rank_limit, factor, 0.0).astype(jnp.bfloat16)
            change = jnp.dot(right_tile, factor, preferred_element_type=jnp.float32)
            pending = pending - jnp.where(active, change, 0.0)
    stacked = jnp.stack(solved)
    columns = lax.all_to_all(stacked, "pr", split_axis=1, concat_axis=2, tiled=True)
    products = jnp.einsum(
        "sbq,fsrb->fsqr", columns, future_left, preferred_element_type=jnp.float32
    )
    products = over_copies(products, "pr")
    future_acc = future_acc - apply_weights(products, future_right, future_ranks)
    return (stacked, future_acc)


def solution(mesh):
    finer = Mesh(mesh.devices.reshape(8, 4, 4, mesh.shape["pr"]), ("tc_0", "tc_1", "tc_2", "pr"))
    in_specs = (
        P(TC, None, "pr"),
        P(TC, None, None),
        P(),
        P(TC, None, None, None),
        P(TC, None, None, None),
        P(TC, None),
        P(TC, None, None, "pr"),
        P(TC, None, None, "pr"),
        P(TC, None),
        P(TC, None, "pr"),
    )
    out_specs = (P(None, None, "pr"), P(TC, None, "pr"))
    return jax.shard_map(local, mesh=finer, in_specs=in_specs, out_specs=out_specs, check_vma=False)
```

profile of v0, /device:TPU:1, one launch (start us, length us, event | category | flops | bytes accessed | tf_op | source)
XLA Modules:
  0.0 229.7 jit_solution(5553572700771871744)
XLA Ops:
  0.7 1.4 fusion.79
  2.7 3.3 %fusion.15 = f32[1536,32]{0,1:T(8,128)S(1)} fusion(bf16[1,1536,1536]{2,1,0:T(8,128)(2,1)} %param.11, f32[1,1536,32]{1,2,0:T(8,128)} %param.10, pred[]{:T(512)S(6)} %eq.18), kind=kOutput, calls=%fused_computation.13 | convolution fusion | flops 151191552 | bytes 5111809 | tf_op jit(solution)/shard_map/dot_general | solution.py:96
  6.1 1.2 copy.102
  7.2 1.2 reshape_reshape.12
  8.4 1.3 copy.139
  9.8 1.5 reshape.72
  11.3 10.0 %all_to_all.83 = f32[4,1,12288]{2,1,0:T(1,128)S(1)} all-to-all(f32[4,1,12288]{2,1,0:T(1,128)S(1)} %reshape.72), channel_id=1, replica_groups=mesh['tc_0'=8,'tc_1'=4,'tc_2'=4,'pr'=2] {'tc_2'}, dimensions={0} | all-to-all | bytes 393216 | tf_op jit(solution)/shard_map/all_to_all | solution.py:44
  21.8 1.1 reduce
  24.1 11.0 %all-to-all-start.1 = ((f32[32,1,384]{2,1,0:T(1,128)}), f32[32,1,384]{2,1,0:T(1,128)S(1)}, u32[]{:S(2)}, u32[]{:S(2)}) async-start(f32[32,1,384]{2,1,0:T(1,128)} %reshape.74), calls=%async_computation.1 | async-start | bytes 98304 | tf_op jit(solution)/shard_map/all_to_all | solution.py:51
  35.9 8.0 %all-to-all-done.1 = f32[32,1,384]{2,1,0:T(1,128)S(1)} async-done(((f32[32,1,384]{2,1,0:T(1,128)}), f32[32,1,384]{2,1,0:T(1,128)S(1)}, u32[]{:S(2)}, u32[]{:S(2)}) %all-to-all-start.1) | async-done | bytes 49184 | tf_op jit(solution)/shard_map/all_to_all | solution.py:51
  45.5 3.9 %all-to-all-start.2 = ((bf16[32,2,192]{2,1,0:T(2,128)(2,1)}), bf16[32,2,192]{2,1,0:T(2,128)(2,1)S(1)}, u32[]{:S(2)}, u32[]{:S(2)}) async-start(bf16[32,2,192]{2,1,0:T(2,128)(2,1)} %reshape.76), calls=%async_computation.2 | async-start | bytes 65536 | tf_op jit(solution)/shard_map/all_to_all | solution.py:19
  53.2 4.8 %all-to-all-done.2 = bf16[32,2,192]{2,1,0:T(2,128)(2,1)S(1)} async-done(((bf16[32,2,192]{2,1,0:T(2,128)(2,1)}), bf16[32,2,192]{2,1,0:T(2,128)(2,1)S(1)}, u32[]{:S(2)}, u32[]{:S(2)}) %all-to-all-start.2) | async-done | bytes 24608 | tf_op jit(solution)/shard_map/all_to_all | solution.py:19
  59.3 3.3 %all-to-all-start.3 = ((bf16[4,2,6144]{2,1,0:T(2,128)(2,1)}), bf16[4,2,6144]{2,1,0:T(2,128)(2,1)S(1)}, u32[]{:S(2)}, u32[]{:S(2)}) async-start(bf16[4,2,6144]{2,1,0:T(2,128)(2,1)} %reshape.78), calls=%async_computation.3 | async-start | bytes 196608 | tf_op jit(solution)/shard_map/all_to_all | solution.py:19
  63.3 3.9 %all-to-all-done.3 = bf16[4,2,6144]{2,1,0:T(2,128)(2,1)S(1)} async-done(((bf16[4,2,6144]{2,1,0:T(2,128)(2,1)}), bf16[4,2,6144]{2,1,0:T(2,128)(2,1)S(1)}, u32[]{:S(2)}, u32[]{:S(2)}) %all-to-all-start.3) | async-done | bytes 98336 | tf_op jit(solution)/shard_map/all_to_all | solution.py:19
  67.9 1.9 fusion.6
  69.8 3.3 %fusion.27 = f32[1536,32]{0,1:T(8,128)S(1)} fusion(bf16[1,1536,1536]{2,1,0:T(8,128)(2,1)} %param.11, f32[1536,32]{0,1:T(8,128)S(1)} %fusion.6, pred[]{:T(512)S(6)} %eq.19), kind=kOutput, calls=%fused_computation.17 | convolution fusion | flops 151191552 | bytes 5111809 | tf_op jit(solution)/shard_map/dot_general | solution.py:96
  73.1 1.2 copy.107
  74.3 1.2 reshape_reshape.13
  75.5 1.3 copy.138
  76.8 1.5 reshape.80
  78.3 7.5 %all_to_all.84 = f32[4,1,12288]{2,1,0:T(1,128)S(1)} all-to-all(f32[4,1,12288]{2,1,0:T(1,128)S(1)} %reshape.80), channel_id=1, replica_groups=mesh['tc_0'=8,'tc_1'=4,'tc_2'=4,'pr'=2] {'tc_2'}, dimensions={0} | all-to-all | bytes 393216 | tf_op jit(solution)/shard_map/all_to_all | solution.py:44
  85.8 1.1 reduce.2
  87.6 12.9 %all_to_all.85 = f32[32,1,384]{2,1,0:T(1,128)S(1)} all-to-all(f32[32,1,384]{2,1,0:T(1,128)S(1)} %reshape.82), channel_id=1, replica_groups=mesh['tc_0'=8,'tc_1'=4,'tc_2'=4,'pr'=2] {'tc_0','tc_1'}, dimensions={0} | all-to-all | bytes 98304 | tf_op jit(solution)/shard_map/all_to_all | solution.py:51
  102.2 3.9 %all-to-all-start.6 = ((bf16[32,2,192]{2,1,0:T(2,128)(2,1)}), bf16[32,2,192]{2,1,0:T(2,128)(2,1)S(1)}, u32[]{:S(2)}, u32[]{:S(2)}) async-start(bf16[32,2,192]{2,1,0:T(2,128)(2,1)} %reshape.84), calls=%async_computation.6 | async-start | bytes 65536 | tf_op jit(solution)/shard_map/all_to_all | solution.py:19
  107.2 7.4 %all-to-all-done.6 = bf16[32,2,192]{2,1,0:T(2,128)(2,1)S(1)} async-done(((bf16[32,2,192]{2,1,0:T(2,128)(2,1)}), bf16[32,2,192]{2,1,0:T(2,128)(2,1)S(1)}, u32[]{:S(2)}, u32[]{:S(2)}) %all-to-all-start.6) | async-done | bytes 24608 | tf_op jit(solution)/shard_map/all_to_all | solution.py:19
  115.9 3.5 %all-to-all-start.7 = ((bf16[4,2,6144]{2,1,0:T(2,128)(2,1)}), bf16[4,2,6144]{2,1,0:T(2,128)(2,1)S(1)}, u32[]{:S(2)}, u32[]{:S(2)}) async-start(bf16[4,2,6144]{2,1,0:T(2,128)(2,1)} %reshape.86), calls=%async_computation.7 | async-start | bytes 196608 | tf_op jit(solution)/shard_map/all_to_all | solution.py:19
  120.1 3.7 %all-to-all-done.7 = bf16[4,2,6144]{2,1,0:T(2,128)(2,1)S(1)} async-done(((bf16[4,2,6144]{2,1,0:T(2,128)(2,1)}), bf16[4,2,6144]{2,1,0:T(2,128)(2,1)S(1)}, u32[]{:S(2)}, u32[]{:S(2)}) %all-to-all-start.7) | async-done | bytes 98336 | tf_op jit(solution)/shard_map/all_to_all | solution.py:19
  124.5 2.6 %fusion.8 = bf16[1536,32]{0,1:T(8,128)(2,1)} fusion(f32[1536,32]{0,1:T(8,128)S(1)} %copy-done.2, bf16[1536,32]{1,0:T(8,128)(2,1)S(1)} %convert_element_type.112, bf16[1,2,1536,200]{2,3,1,0:T(8,128)(2,1)} %param.13, s32[]{:T(128)S(6)} %min.8, bf16[1,2,1536,200]{2,3,1,0:T(8,128)(2,1)} %param.14, pred[]{:T(512)S(6)} %and.10, ...), kind=kOutput, calls=%fused_computation.10 | convolution fusion | flops 39481856 | bytes 1623752 | tf_op jit(solution)/shard_map/dot_general | solution.py:117
  127.0 3.3 %fusion.39 = f32[1536,32]{0,1:T(8,128)S(1)} fusion(bf16[1536,32]{0,1:T(8,128)(2,1)} %fusion.8, bf16[1,1536,1536]{2,1,0:T(8,128)(2,1)} %param.11, pred[]{:T(512)S(6)} %eq.15), kind=kOutput, calls=%fused_computation.21 | convolution fusion | flops 151142400 | bytes 5013505 | tf_op jit(solution)/shard_map/dot_general | solution.py:96
  130.3 1.2 copy.112
  131.6 2.2 reshape_reshape.14
  133.7 2.6 %copy.137 = f32[4,32,12,32]{3,1,2,0:T(8,128)} copy(f32[4,32,12,32]{3,2,0,1:T(8,128)} %bitcast.126) | data formatting | bytes 393216 | tf_op jit(solution)/shard_map/transpose | solution.py:39
  136.3 1.5 reshape.88
  137.8 7.5 %all_to_all.86 = f32[4,1,12288]{2,1,0:T(1,128)S(1)} all-to-all(f32[4,1,12288]{2,1,0:T(1,128)S(1)} %reshape.88), channel_id=1, replica_groups=mesh['tc_0'=8,'tc_1'=4,'tc_2'=4,'pr'=2] {'tc_2'}, dimensions={0} | all-to-all | bytes 393216 | tf_op jit(solution)/shard_map/all_to_all | solution.py:44
  146.5 1.2 reshape.89
  147.7 1.2 bitcast_reduce_fusion
  149.2 11.7 %all_to_all.87 = f32[32,1,384]{2,1,0:T(1,128)S(1)} all-to-all(f32[32,1,384]{2,1,0:T(1,128)S(1)} %reshape.90), channel_id=1, replica_groups=mesh['tc_0'=8,'tc_1'=4,'tc_2'=4,'pr'=2] {'tc_0','tc_1'}, dimensions={0} | all-to-all | bytes 98304 | tf_op jit(solution)/shard_map/all_to_all | solution.py:51
  161.9 11.6 %all_to_all.88 = bf16[32,2,192]{2,1,0:T(2,128)(2,1)S(1)} all-to-all(bf16[32,2,192]{2,1,0:T(2,128)(2,1)S(1)} %reshape.92), channel_id=1, replica_groups=mesh['tc_0'=8,'tc_1'=4,'tc_2'=4,'pr'=2] {'tc_0','tc_1'}, dimensions={0} | all-to-all | bytes 49152 | tf_op jit(solution)/shard_map/all_to_all | solution.py:19
  174.8 3.3 %all-to-all-start.11 = ((bf16[4,2,6144]{2,1,0:T(2,128)(2,1)}), bf16[4,2,6144]{2,1,0:T(2,128)(2,1)S(1)}, u32[]{:S(2)}, u32[]{:S(2)}) async-start(bf16[4,2,6144]{2,1,0:T(2,128)(2,1)} %reshape.94), calls=%async_computation.11 | async-start | bytes 196608 | tf_op jit(solution)/shard_map/all_to_all | solution.py:19
  179.2 3.8 %all-to-all-done.11 = bf16[4,2,6144]{2,1,0:T(2,128)(2,1)S(1)} async-done(((bf16[4,2,6144]{2,1,0:T(2,128)(2,1)}), bf16[4,2,6144]{2,1,0:T(2,128)(2,1)S(1)}, u32[]{:S(2)}, u32[]{:S(2)}) %all-to-all-start.11) | async-done | bytes 98336 | tf_op jit(solution)/shard_map/all_to_all | solution.py:19
  187.6 8.2 %copy.136 = bf16[3,1536,32]{2,0,1:T(4,128)(2,1)} copy(bf16[3,1536,32]{2,1,0:T(8,128)(2,1)S(1)} %constant_dynamic-update-slice_fusion) | data formatting | bytes 589824 | tf_op jit(solution)/shard_map/stack | solution.py:119
  195.8 2.3 reshape.96
  198.1 18.6 %all_to_all.89 = bf16[2,2,36864]{2,1,0:T(2,128)(2,1)} all-to-all(bf16[2,2,36864]{2,1,0:T(2,128)(2,1)S(1)} %reshape.96), channel_id=1, replica_groups=mesh['tc_0'=8,'tc_1'=4,'tc_2'=4,'pr'=2] {'pr'}, dimensions={0} | all-to-all | bytes 589824 | tf_op jit(solution)/shard_map/all_to_all | solution.py:120
  216.6 2.0 reshape.97
  218.6 1.8 copy.127
  221.5 2.2 fusion.44
  223.8 4.5 %all_to_all.90 = f32[2,2,3,64,200]{4,3,2,1,0:T(8,128)S(1)} all-to-all(f32[2,2,3,64,200]{4,3,2,1,0:T(8,128)S(1)} %broadcast_in_dim.91), channel_id=1, replica_groups=mesh['tc_0'=8,'tc_1'=4,'tc_2'=4,'pr'=2] {'pr'}, dimensions={0} | all-to-all | bytes 1228800 | tf_op jit(solution)/shard_map/all_to_all | solution.py:19
  228.4 1.3 fusion.47
  (82 shorter events, 23.0 us)
Async XLA Ops:
  0.6 227.7 %copy-start = (bf16[2,3,200,768]{3,2,1,0:T(8,128)(2,1)S(1)}, bf16[2,3,200,768]{3,2,1,0:T(8,128)(2,1)}, u32[]{:S(2)}) copy-start(bf16[2,3,200,768]{3,2,1,0:T(8,128)(2,1)} %param.17) | copy-start | bytes 5529604
  21.8 13.4 %copy-start.5 = (s32[3]{0:T(128)S(1)}, s32[3]{0:T(128)}, u32[]{:S(2)}) copy-start(s32[3]{0:T(128)} %param.12) | copy-start | bytes 40
  23.2 29.4 %copy-start.7 = (s32[1,2]{1,0:T(1,128)S(1)}, s32[1,2]{1,0:T(1,128)}, u32[]{:S(2)}) copy-start(s32[1,2]{1,0:T(1,128)} %param.15) | copy-start | bytes 28
  24.1 19.8 %all-to-all-start.1 = ((f32[32,1,384]{2,1,0:T(1,128)}), f32[32,1,384]{2,1,0:T(1,128)S(1)}, u32[]{:S(2)}, u32[]{:S(2)}) async-start(f32[32,1,384]{2,1,0:T(1,128)} %reshape.74), calls=%async_computation.1 | async-start | bytes 98304 | tf_op jit(solution)/shard_map/all_to_all | solution.py:51
  45.5 12.5 %all-to-all-start.2 = ((bf16[32,2,192]{2,1,0:T(2,128)(2,1)}), bf16[32,2,192]{2,1,0:T(2,128)(2,1)S(1)}, u32[]{:S(2)}, u32[]{:S(2)}) async-start(bf16[32,2,192]{2,1,0:T(2,128)(2,1)} %reshape.76), calls=%async_computation.2 | async-start | bytes 65536 | tf_op jit(solution)/shard_map/all_to_all | solution.py:19
  59.3 7.9 %all-to-all-start.3 = ((bf16[4,2,6144]{2,1,0:T(2,128)(2,1)}), bf16[4,2,6144]{2,1,0:T(2,128)(2,1)S(1)}, u32[]{:S(2)}, u32[]{:S(2)}) async-start(bf16[4,2,6144]{2,1,0:T(2,128)(2,1)} %reshape.78), calls=%async_computation.3 | async-start | bytes 196608 | tf_op jit(solution)/shard_map/all_to_all | solution.py:19
  62.6 5.2 %copy-start.3 = (f32[1,1536,32]{1,2,0:T(8,128)S(1)}, f32[1,1536,32]{1,2,0:T(8,128)}, u32[]{:S(2)}) copy-start(f32[1,1536,32]{1,2,0:T(8,128)} %param.10) | copy-start | bytes 589828
  69.8 3.3 %copy-start.1 = (f32[1536,32]{0,1:T(8,128)}, f32[1536,32]{0,1:T(8,128)S(1)}, u32[]{:S(2)}) copy-start(f32[1536,32]{0,1:T(8,128)S(1)} %fusion.6) | copy-start | bytes 589828
  102.2 12.5 %all-to-all-start.6 = ((bf16[32,2,192]{2,1,0:T(2,128)(2,1)}), bf16[32,2,192]{2,1,0:T(2,128)(2,1)S(1)}, u32[]{:S(2)}, u32[]{:S(2)}) async-start(bf16[32,2,192]{2,1,0:T(2,128)(2,1)} %reshape.84), calls=%async_computation.6 | async-start | bytes 65536 | tf_op jit(solution)/shard_map/all_to_all | solution.py:19
  115.9 7.9 %all-to-all-start.7 = ((bf16[4,2,6144]{2,1,0:T(2,128)(2,1)}), bf16[4,2,6144]{2,1,0:T(2,128)(2,1)S(1)}, u32[]{:S(2)}, u32[]{:S(2)}) async-start(bf16[4,2,6144]{2,1,0:T(2,128)(2,1)} %reshape.86), calls=%async_computation.7 | async-start | bytes 196608 | tf_op jit(solution)/shard_map/all_to_all | solution.py:19
  119.4 5.0 %copy-start.2 = (f32[1536,32]{0,1:T(8,128)S(1)}, f32[1536,32]{0,1:T(8,128)}, u32[]{:S(2)}) copy-start(f32[1536,32]{0,1:T(8,128)} %copy-done.1) | copy-start | bytes 589828
  174.8 8.2 %all-to-all-start.11 = ((bf16[4,2,6144]{2,1,0:T(2,128)(2,1)}), bf16[4,2,6144]{2,1,0:T(2,128)(2,1)S(1)}, u32[]{:S(2)}, u32[]{:S(2)}) async-start(bf16[4,2,6144]{2,1,0:T(2,128)(2,1)} %reshape.94), calls=%async_computation.11 | async-start | bytes 196608 | tf_op jit(solution)/shard_map/all_to_all | solution.py:19
  223.8 4.6 %copy-start.4 = (f32[2,64,768]{2,1,0:T(8,128)S(1)}, f32[2,64,768]{2,1,0:T(8,128)}, u32[]{:S(2)}) copy-start(f32[2,64,768]{2,1,0:T(8,128)} %param.19) | copy-start | bytes 1179652
  223.8 4.6 %copy-start.6 = (s32[2,3]{1,0:T(2,128)S(1)}, s32[2,3]{1,0:T(2,128)}, u32[]{:S(2)}) copy-start(s32[2,3]{1,0:T(2,128)} %param.18) | copy-start | bytes 76
where the time goes:
time: 231 us; the launch traced here: 230 us
  blocking collectives  84.4 us (37%)
  local copies, waits for them, and re-layouts  51.5 us (22%)
  waiting for transfers between devices  31.7 us (14%)
  starting transfers between devices  28.8 us (12%)
  matrix products  17.9 us (8%)
  other arithmetic  9.7 us (4%)
  between operations  5.64 us (2%)
    all_to_all x3, blocking collectives, sum_at_owner(): lax.all_to_all(pieces, axis, split_axis=0, concat_axis=0, tiled=True)  25.1 us
    all_to_all x2, blocking collectives, summed_rows(): return jnp.sum(lax.all_to_all(own, far, 0, 0, tiled=True), axis=0)  24.7 us
    all_to_all x5, waiting for transfers between devices, sent_to_all(): lax.all_to_all(jnp.broadcast_to(shard[None], (count, *shard.shape)), axis...  23.7 us
    unnamed x48, local copies, waits for them, and re-layouts  20.9 us
    all_to_all x1, blocking collectives, local(): lax.all_to_all(stacked, 'pr', split_axis=1, concat_axis=2, tiled=True)  18.6 us
    all_to_all x5, starting transfers between devices, sent_to_all(): lax.all_to_all(jnp.broadcast_to(shard[None], (count, *shard.shape)), axis...  17.8 us
    all_to_all x2, blocking collectives, sent_to_all(): lax.all_to_all(jnp.broadcast_to(shard[None], (count, *shard.shape)), axis...  16.1 us
    all_to_all x1, starting transfers between devices, summed_rows(): return jnp.sum(lax.all_to_all(own, far, 0, 0, tiled=True), axis=0)  11 us
  transfers between devices with their start and end apart: 6, of which 6 were waited for; matrix products, arithmetic and copies ran while one was open for 2% of the time, Pallas kernels for 0%

commit v1 on v0

v1 whole, which is shorter than its diff:
```python
import functools

import jax
import jax.numpy as jnp
from jax import lax
from jax.experimental import pallas as pl
from jax.experimental.pallas import tpu as pltpu
from jax.sharding import Mesh
from jax.sharding import PartitionSpec as P

TC = ("tz", "tx", "ty")
MESH = pl.DeviceIdType.MESH
NZ, NX, NY, NC = 8, 4, 4, 2
PIV, B, PROBES, R = 3, 1536, 32, 200
GROUP, COLS = PROBES // NX, B // NY
BLOCK = 256


def ring_distance(step, size):
    return min(step, size - step)


PLANE = sorted(
    ((dx, dy) for dx in range(NX) for dy in range(NY) if (dx, dy) != (0, 0)),
    key=lambda d: -(ring_distance(d[0], NX) + ring_distance(d[1], NY)),
)
COLUMN = sorted(range(1, NZ), key=lambda d: -ring_distance(d, NZ))


def matmul(a, b):
    return lax.dot_general(a, b, (((1,), (0,)), ((), ())), preferred_element_type=jnp.float32)


def matmul_t(a, b):
    return lax.dot_general(a, b, (((1,), (1,)), ((), ())), preferred_element_type=jnp.float32)


def kernel(
    owner_ref, coupling_ranks_ref, future_ranks_ref,
    rhs_ref, inverse_ref, left_ref, right_ref, future_left_ref, future_right_ref, future_rhs_ref,
    solved_ref, future_out_ref,
    inverse, rhs, left, right, future_left, future_right, future, gain, acc, block,
    rs_send, rs_recv, z_send, z_recv, whole,
    load_sem, panel_sem, out_sem, swap_sem,
    rs_send_sem, rs_recv_sem, z_send_sem, z_recv_sem,
    own_send_sem, own_recv_sem, far_send_sem, far_recv_sem,
):
    mz, mx, my, mc = (lax.axis_index(name) for name in (*TC, "pr"))
    me = (mz * NX + mx) * NY + my
    other = 1 - mc

    def shifted(dx, dy):
        return lax.rem(mx + dx, NX), lax.rem(my + dy, NY)

    rhs_load = pltpu.make_async_copy(rhs_ref, rhs, load_sem.at[0])
    rhs_load.start()
    panels = []
    for k in range(B // BLOCK):
        rows, columns = pl.ds(k * BLOCK, BLOCK), pl.ds(0, (k + 1) * BLOCK)
        panel = pltpu.make_async_copy(
            inverse_ref.at[rows, columns], inverse.at[rows, columns], panel_sem.at[k]
        )
        panel.start()
        panels.append(panel)

    barrier = pltpu.get_barrier_semaphore()
    greeted = 0
    for dx, dy in PLANE:
        px, py = shifted(dx, dy)
        for core in (mc, other):
            pl.semaphore_signal(barrier, 1, device_id=(mz, px, py, core), device_id_type=MESH)
            greeted += 1
    for dz in COLUMN:
        pz = lax.rem(mz + dz, NZ)
        pl.semaphore_signal(barrier, 1, device_id=(pz, mx, my, mc), device_id_type=MESH)
        greeted += 1
    pl.semaphore_signal(barrier, 1, device_id=(mz, mx, my, other), device_id_type=MESH)
    greeted += 1

    loads = [
        pltpu.make_async_copy(right_ref, right, load_sem.at[1]),
        pltpu.make_async_copy(left_ref, left, load_sem.at[2]),
        pltpu.make_async_copy(future_left_ref, future_left.at[mc], load_sem.at[3]),
        pltpu.make_async_copy(future_right_ref, future_right, load_sem.at[4]),
        pltpu.make_async_copy(future_rhs_ref, future, load_sem.at[5]),
    ]

    rhs_load.wait()
    start = rhs[...].astype(jnp.bfloat16)
    sums = [None] * (B // BLOCK)
    for k in range(B // BLOCK):
        panels[k].wait()
        piece = start[:, k * BLOCK : (k + 1) * BLOCK]
        for c in range(k + 1):
            term = matmul(piece, inverse[k * BLOCK : (k + 1) * BLOCK, c * BLOCK : (c + 1) * BLOCK])
            sums[c] = term if sums[c] is None else sums[c] + term
    for c in range(B // BLOCK):
        acc[:, c * BLOCK : (c + 1) * BLOCK] = sums[c]
    for load in loads:
        load.start()
    pl.semaphore_wait(barrier, greeted)

    swap = pltpu.make_async_remote_copy(
        src_ref=future_left_ref,
        dst_ref=future_left.at[mc],
        send_sem=swap_sem.at[0],
        recv_sem=swap_sem.at[1],
        device_id=(mz, mx, my, other),
        device_id_type=MESH,
    )
    swap_in = pltpu.make_async_remote_copy(
        src_ref=future_left_ref,
        dst_ref=future_left.at[other],
        send_sem=swap_sem.at[0],
        recv_sem=swap_sem.at[1],
        device_id=(mz, mx, my, other),
        device_id_type=MESH,
    )

    own_pivot = jnp.int32(0)
    holds = jnp.int32(0)
    for p in range(PIV):
        mine = (owner_ref[p] == me).astype(jnp.int32)
        own_pivot = own_pivot + mine * p
        holds = holds + mine
    rank_ids = lax.broadcasted_iota(jnp.int32, (PROBES, R), 1)
    future_rank_ids = lax.broadcasted_iota(jnp.int32, (NC * PROBES, R), 1)

    sent = []

    def send(src, dst, send_sem, recv_sem, device):
        copy = pltpu.make_async_remote_copy(
            src_ref=src, dst_ref=dst, send_sem=send_sem, recv_sem=recv_sem,
            device_id=device, device_id_type=MESH,
        )
        copy.start()
        sent.append(copy)

    def receive(dst, send_sem, recv_sem):
        pltpu.make_async_remote_copy(
            src_ref=dst, dst_ref=dst, send_sem=send_sem, recv_sem=recv_sem,
            device_id=(mz, mx, my, other), device_id_type=MESH,
        ).wait_recv()

    def assembled(i, core):
        columns = [
            whole[i, core, :, g].astype(jnp.float32).reshape(PROBES, COLS) for g in range(NY)
        ]
        return jnp.concatenate(columns, axis=1).astype(jnp.bfloat16)

    def make_gain():
        loads[0].wait()
        for c in range(B // BLOCK):
            columns = pl.ds(c * BLOCK, BLOCK)
            below = pl.ds(c * BLOCK, B - c * BLOCK)
            for j in range(PIV - 1):
                gain[j, :, columns] = matmul(right[j, :, below], inverse[below, columns]).astype(jnp.bfloat16)

    def apply_future(i, p):
        for k, (dx, dy) in enumerate(PLANE):
            px, py = shifted(NX - dx, NY - dy)
            receive(whole.at[i, other, px, py], far_send_sem.at[i, k], far_recv_sem.at[i, k])
        receive(whole.at[i, other, mx, my], far_send_sem.at[i, len(PLANE)], far_recv_sem.at[i, len(PLANE)])
        both = jnp.concatenate([assembled(i, 0), assembled(i, 1)], axis=0)
        half = B // NC
        for f in range(2):
            weights = matmul_t(both[:, :half], future_left[0, f, p]) + matmul_t(
                both[:, half:], future_left[1, f, p]
            )
            weights = jnp.where(future_rank_ids < future_ranks_ref[f, p], weights, 0.0)
            future[f] = future[f] - matmul(weights.astype(jnp.bfloat16), future_right[f, p])

    outs = []
    for i, p in enumerate(reversed(range(PIV))):
        is_root = owner_ref[p] == me
        masked = jnp.where(is_root, acc[...], 0.0).reshape(NX, GROUP, B).astype(jnp.bfloat16)
        for g in range(NY):
            rs_send[i, :, g] = masked[:, :, g * COLS : (g + 1) * COLS]
        for k, (dx, dy) in enumerate(PLANE):
            px, py = shifted(dx, dy)
            send(
                rs_send.at[i, px, py], rs_recv.at[i, k],
                rs_send_sem.at[i, k], rs_recv_sem.at[i, k], (mz, px, py, mc),
            )
        if i == 0:
            swap.start()
            make_gain()
            loads[1].wait()
        else:
            if i == 1:
                swap_in.wait_recv()
                for load in loads[2:]:
                    load.wait()
            apply_future(i - 1, p + 1)

        part = rs_send[i, mx, my].astype(jnp.float32)
        for k in range(len(PLANE)):
            receive(rs_recv.at[i, k], rs_send_sem.at[i, k], rs_recv_sem.at[i, k])
            part = part + rs_recv[i, k].astype(jnp.float32)
        z_send[i] = part.astype(jnp.bfloat16)
        for k, dz in enumerate(COLUMN):
            send(
                z_send.at[i], z_recv.at[i, k], z_send_sem.at[i, k], z_recv_sem.at[i, k],
                (lax.rem(mz + dz, NZ), mx, my, mc),
            )
        for k in range(len(COLUMN)):
            receive(z_recv.at[i, k], z_send_sem.at[i, k], z_recv_sem.at[i, k])
            part = part + z_recv[i, k].astype(jnp.float32)
        whole[i, mc, mx, my] = part.astype(jnp.bfloat16)
        piece = whole.at[i, mc, mx, my]
        for k, (dx, dy) in enumerate(PLANE):
            px, py = shifted(dx, dy)
            send(piece, piece, own_send_sem.at[i, k], own_recv_sem.at[i, k], (mz, px, py, mc))
        for k, (dx, dy) in enumerate(PLANE):
            px, py = shifted(dx, dy)
            send(piece, piece, far_send_sem.at[i, k], far_recv_sem.at[i, k], (mz, px, py, other))
        last = len(PLANE)
        send(piece, piece, far_send_sem.at[i, last], far_recv_sem.at[i, last], (mz, mx, my, other))
        for k, (dx, dy) in enumerate(PLANE):
            px, py = shifted(NX - dx, NY - dy)
            receive(whole.at[i, mc, px, py], own_send_sem.at[i, k], own_recv_sem.at[i, k])
        columns = assembled(i, mc)
        block[i] = columns
        out = pltpu.make_async_copy(block.at[i], solved_ref.at[p], out_sem.at[i])
        out.start()
        outs.append(out)
        if p > 0:
            entry = jnp.clip(p - own_pivot - 1, 0, PIV - 2)
            active = holds * (own_pivot < p).astype(jnp.int32)
            factor = matmul_t(columns, left[entry])
            factor = jnp.where(rank_ids < coupling_ranks_ref[0, entry] * active, factor, 0.0)
            acc[...] = acc[...] - matmul(factor.astype(jnp.bfloat16), gain[entry])
    apply_future(PIV - 1, 0)
    out = pltpu.make_async_copy(future, future_out_ref, out_sem.at[PIV])
    out.start()
    outs.append(out)
    for copy in sent:
        copy.wait_send()
    swap.wait_send()
    for out in outs:
        out.wait()


def local(
    pivot_rhs, pivot_inverse, pivot_owner, coupling_left, coupling_right, coupling_ranks,
    future_left, future_right, future_ranks, future_rhs,
):
    smem = pl.BlockSpec(memory_space=pltpu.SMEM)
    hbm = pl.BlockSpec(memory_space=pl.ANY)
    plane, column = len(PLANE), len(COLUMN)
    dma = pltpu.SemaphoreType.DMA
    bf16, f32 = jnp.bfloat16, jnp.float32
    solved, future_out = pl.pallas_call(
        kernel,
        out_shape=(
            jax.ShapeDtypeStruct((PIV, PROBES, B), bf16),
            jax.ShapeDtypeStruct(future_rhs.shape, f32),
        ),
        in_specs=[smem] * 3 + [hbm] * 7,
        out_specs=(hbm, hbm),
        scratch_shapes=[
            pltpu.VMEM((B, B), bf16),
            pltpu.VMEM((PROBES, B), f32),
            pltpu.VMEM((PIV - 1, R, B), bf16),
            pltpu.VMEM((PIV - 1, R, B), bf16),
            pltpu.VMEM((NC, *future_left.shape), bf16),
            pltpu.VMEM(future_right.shape, bf16),
            pltpu.VMEM(future_rhs.shape, f32),
            pltpu.VMEM((PIV - 1, R, B), bf16),
            pltpu.VMEM((PROBES, B), f32),
            pltpu.VMEM((PIV, PROBES, B), bf16),
            pltpu.VMEM((PIV, NX, NY, GROUP, COLS), bf16),
            pltpu.VMEM((PIV, plane, GROUP, COLS), bf16),
            pltpu.VMEM((PIV, GROUP, COLS), bf16),
            pltpu.VMEM((PIV, column, GROUP, COLS), bf16),
            pltpu.VMEM((PIV, NC, NX, NY, GROUP, COLS), bf16),
            dma((6,)),
            dma((B // BLOCK,)),
            dma((PIV + 1,)),
            dma((2,)),
            dma((PIV, plane)),
            dma((PIV, plane)),
            dma((PIV, column)),
            dma((PIV, column)),
            dma((PIV, plane)),
            dma((PIV, plane)),
            dma((PIV, plane + 1)),
            dma((PIV, plane + 1)),
        ],
        compiler_params=pltpu.CompilerParams(collective_id=0, has_side_effects=True),
    )(
        pivot_owner,
        coupling_ranks,
        future_ranks,
        pivot_rhs[0].T,
        pivot_inverse[0],
        coupling_left[0].swapaxes(1, 2),
        coupling_right[0].swapaxes(1, 2),
        future_left,
        future_right,
        future_rhs,
    )
    return solved.swapaxes(1, 2), future_out


def solution(mesh):
    finer = Mesh(mesh.devices.reshape(NZ, NX, NY, NC), (*TC, "pr"))
    in_specs = (
        P(TC, None, "pr"),
        P(TC, None, None),
        P(),
        P(TC, None, None, None),
        P(TC, None, None, None),
        P(TC, None),
        P(TC, None, None, "pr"),
        P(TC, None, None, "pr"),
        P(TC, None),
        P(TC, None, "pr"),
    )
    out_specs = (P(None, None, "pr"), P(TC, None, "pr"))
    return jax.shard_map(local, mesh=finer, in_specs=in_specs, out_specs=out_specs, check_vma=False)
```

time: 231 us -> 64.7 us (0.28)
  blocking collectives: 84.4 us -> 0 us
  Pallas kernels: 0 us -> 60.4 us
  local copies, waits for them, and re-layouts: 51.5 us -> 3.46 us
  waiting for transfers between devices: 31.7 us -> 0 us
  starting transfers between devices: 28.8 us -> 0 us
  matrix products: 17.9 us -> 0 us
  other arithmetic: 9.7 us -> 0 us
  between operations: 5.64 us -> 0.64 us
    all_to_all x8 -> x0, blocking collectives: 84.4 us -> none  [the longest x3 25.1 us: sum_at_owner(): lax.all_to_all(pieces, axis, split_axis=0, concat_axis=0, tiled=True)]
    pallas_call x0 -> x1, Pallas kernels: none -> 60.4 us  [local(): pl.pallas_call(kernel, out_shape=(jax.ShapeDtypeStruct((PIV, PROBES, B),...]
    all_to_all x6 -> x0, waiting for transfers between devices: 31.7 us -> none  [the longest x5 23.7 us: sent_to_all(): lax.all_to_all(jnp.broadcast_to(shard[None], (count, *shard.shape)), axis...]
    all_to_all x6 -> x0, starting transfers between devices: 28.8 us -> none  [the longest x5 17.8 us: sent_to_all(): lax.all_to_all(jnp.broadcast_to(shard[None], (count, *shard.shape)), axis...]
    dot_general x7 -> x0, matrix products: 17.9 us -> none  [the longest x3 9.94 us: local(): lax.dot_general(inverse_tile, pivot_in, (((0,), (0,)), ((), ())), preferr...]
    unnamed x48 -> x2, local copies, waits for them, and re-layouts: 20.9 us -> 3.46 us
    another operation x5 -> x0, local copies, waits for them, and re-layouts: 12.8 us -> none  [the longest x2 8.25 us: local(): stacked = jnp.stack(solved)]
    all_to_all x6 -> x0, other arithmetic: 5.43 us -> none  [the longest x3 3.35 us: sum_at_owner(): lax.all_to_all(pieces, axis, split_axis=0, concat_axis=0, tiled=True)]
  transfers between devices with their start and end apart: 6 -> 0, of which waited for: 6 -> 0; matrix products, arithmetic and copies ran while one was open for 2% -> 0% of each run, Pallas kernels for 0% -> 0%
where the time goes in v1:
time: 64.7 us; the launch traced here: 64.5 us
  Pallas kernels  60.4 us (93%)
  local copies, waits for them, and re-layouts  3.46 us (5%)
    pallas_call x1, Pallas kernels, local(): pl.pallas_call(kernel, out_shape=(jax.ShapeDtypeStruct((PIV, PROBES, B),...  60.4 us
    unnamed x2, local copies, waits for them, and re-layouts  3.46 us

profile of v1, /device:TPU:1, one launch (start us, length us, event | category | flops | bytes accessed | tf_op | source)
XLA Modules:
  0.0 64.5 jit_solution(1471958295118559240)
XLA Ops:
  0.6 60.4 %shard_map.113 = (bf16[3,32,1536]{2,1,0:T(8,128)(2,1)}, f32[2,64,768]{2,1,0:T(8,128)}) custom-call(s32[3]{0:T(128)} %owner_ref.1, s32[1,2]{1,0:T(1,128)} %coupling_ranks_ref.1, s32[2,3]{1,0:T(2,128)} %future_ranks_ref.1, f32[32,1536]{1,0:T(8,128)} %bitcast.15, bf16[1536,1536]{1,0:T(8,128)(2,1)} %bitcast.11, bf16[2,200,1536]{2,1,0:T(8,128)(2,1)} %bitcast.12, ...), custom_call_target="tpu_custom_call" | custom-call | tf_op jit(solution)/shard_map/pallas_call | solution.py:253
  61.0 1.7 %copy.14 = bf16[3,1536,32]{1,2,0:T(8,128)(2,1)} copy(bf16[3,1536,32]{1,2,0:T(8,128)(2,1)} %bitcast.14) | data formatting | bytes 589824
  62.7 1.8 %copy.15 = f32[2,64,768]{2,1,0:T(8,128)} copy(f32[2,64,768]{2,1,0:T(8,128)} %get-tuple-element.9) | data formatting | bytes 786432

commit v2 on v1

--- a/solution.py
+++ b/solution.py
@@ -13,6 +13,7 @@
 NZ, NX, NY, NC = 8, 4, 4, 2
 PIV, B, PROBES, R = 3, 1536, 32, 200
 GROUP, COLS = PROBES // NX, B // NY
+RANKS = 56
 BLOCK = 256
 
 
@@ -25,6 +26,7 @@
     key=lambda d: -(ring_distance(d[0], NX) + ring_distance(d[1], NY)),
 )
 COLUMN = sorted(range(1, NZ), key=lambda d: -ring_distance(d, NZ))
+RING = (2, 1, 3)
 
 
 def matmul(a, b):
@@ -41,9 +43,12 @@
     solved_ref, future_out_ref,
     inverse, rhs, left, right, future_left, future_right, future, gain, acc, block,
     rs_send, rs_recv, z_send, z_recv, whole,
+    pair_send, pair_recv, pair, rest_send, rest_recv, f_send, f_recv,
     load_sem, panel_sem, out_sem, swap_sem,
     rs_send_sem, rs_recv_sem, z_send_sem, z_recv_sem,
     own_send_sem, own_recv_sem, far_send_sem, far_recv_sem,
+    pair_send_sem, pair_recv_sem, near_send_sem, near_recv_sem, cross_send_sem, cross_recv_sem,
+    rest_send_sem, rest_recv_sem, f_send_sem, f_recv_sem,
 ):
     mz, mx, my, mc = (lax.axis_index(name) for name in (*TC, "pr"))
     me = (mz * NX + mx) * NY + my
@@ -85,6 +90,8 @@
         pltpu.make_async_copy(future_rhs_ref, future, load_sem.at[5]),
     ]
 
+    for load in loads[:2]:
+        load.start()
     rhs_load.wait()
     start = rhs[...].astype(jnp.bfloat16)
     sums = [None] * (B // BLOCK)
@@ -96,7 +103,7 @@
             sums[c] = term if sums[c] is None else sums[c] + term
     for c in range(B // BLOCK):
         acc[:, c * BLOCK : (c + 1) * BLOCK] = sums[c]
-    for load in loads:
+    for load in loads[2:]:
         load.start()
     pl.semaphore_wait(barrier, greeted)
 
@@ -148,13 +155,54 @@
         ]
         return jnp.concatenate(columns, axis=1).astype(jnp.bfloat16)
 
-    def make_gain():
-        loads[0].wait()
+    def make_gain(j):
         for c in range(B // BLOCK):
             columns = pl.ds(c * BLOCK, BLOCK)
             below = pl.ds(c * BLOCK, B - c * BLOCK)
-            for j in range(PIV - 1):
-                gain[j, :, columns] = matmul(right[j, :, below], inverse[below, columns]).astype(jnp.bfloat16)
+            gain[j, :, columns] = matmul(right[j, :, below], inverse[below, columns]).astype(jnp.bfloat16)
+
+    def spread_pair():
+        limit = jnp.where(owner_ref[0] == me, coupling_ranks_ref[0, 0], 0)
+        for x in range(NX):
+            count = min(RANKS, R - x * RANKS)
+            rows = pl.ds(x * RANKS, count)
+            ids = lax.broadcasted_iota(jnp.int32, (count, COLS), 0) + x * RANKS
+            for y in range(NY):
+                columns = pl.ds(y * COLS, COLS)
+                value = jnp.where(
+                    mc == 0, left[0, rows, columns].astype(jnp.float32), gain[0, rows, columns].astype(jnp.float32)
+                )
+                pair_send[x, y, pl.ds(0, count)] = jnp.where(ids < limit, value, 0.0).astype(jnp.bfloat16)
+                if count < RANKS:
+                    pair_send[x, y, pl.ds(count, RANKS - count)] = jnp.zeros((RANKS - count, COLS), jnp.bfloat16)
+        for k, (dx, dy) in enumerate(PLANE):
+            px, py = shifted(dx, dy)
+            send(
+                pair_send.at[px, py], pair_recv.at[k], pair_send_sem.at[k], pair_recv_sem.at[k],
+                (mz, px, py, mc),
+            )
+
+    def share_pair():
+        total = pair_send[mx, my].astype(jnp.float32)
+        for k in range(len(PLANE)):
+            receive(pair_recv.at[k], pair_send_sem.at[k], pair_recv_sem.at[k])
+            total = total + pair_recv[k].astype(jnp.float32)
+        pair[mc, mx] = total.astype(jnp.bfloat16)
+        piece = pair.at[mc, mx]
+        for k, d in enumerate(RING):
+            px = lax.rem(mx + d, NX)
+            send(piece, piece, near_send_sem.at[k], near_recv_sem.at[k], (mz, px, my, mc))
+            send(piece, piece, cross_send_sem.at[k], cross_recv_sem.at[k], (mz, px, my, other))
+        last = len(RING)
+        send(piece, piece, cross_send_sem.at[last], cross_recv_sem.at[last], (mz, mx, my, other))
+
+    def take_pair():
+        for k, d in enumerate(RING):
+            px = lax.rem(mx + NX - d, NX)
+            receive(pair.at[mc, px], near_send_sem.at[k], near_recv_sem.at[k])
+            receive(pair.at[other, px], cross_send_sem.at[k], cross_recv_sem.at[k])
+        last = len(RING)
+        receive(pair.at[other, mx], cross_send_sem.at[last], cross_recv_sem.at[last])
 
     def apply_future(i, p):
         for k, (dx, dy) in enumerate(PLANE):
@@ -170,10 +218,8 @@
             weights = jnp.where(future_rank_ids < future_ranks_ref[f, p], weights, 0.0)
             future[f] = future[f] - matmul(weights.astype(jnp.bfloat16), future_right[f, p])
 
-    outs = []
-    for i, p in enumerate(reversed(range(PIV))):
-        is_root = owner_ref[p] == me
-        masked = jnp.where(is_root, acc[...], 0.0).reshape(NX, GROUP, B).astype(jnp.bfloat16)
+    def scatter(i, p):
+        masked = jnp.where(owner_ref[p] == me, acc[...], 0.0).reshape(NX, GROUP, B).astype(jnp.bfloat16)
         for g in range(NY):
             rs_send[i, :, g] = masked[:, :, g * COLS : (g + 1) * COLS]
         for k, (dx, dy) in enumerate(PLANE):
@@ -182,31 +228,31 @@
                 rs_send.at[i, px, py], rs_recv.at[i, k],
                 rs_send_sem.at[i, k], rs_recv_sem.at[i, k], (mz, px, py, mc),
             )
-        if i == 0:
-            swap.start()
-            make_gain()
-            loads[1].wait()
-        else:
-            if i == 1:
-                swap_in.wait_recv()
-                for load in loads[2:]:
-                    load.wait()
-            apply_future(i - 1, p + 1)
-
+
+    def scattered(i):
         part = rs_send[i, mx, my].astype(jnp.float32)
         for k in range(len(PLANE)):
             receive(rs_recv.at[i, k], rs_send_sem.at[i, k], rs_recv_sem.at[i, k])
             part = part + rs_recv[i, k].astype(jnp.float32)
+        return part
+
+    def send_column(i, part):
         z_send[i] = part.astype(jnp.bfloat16)
         for k, dz in enumerate(COLUMN):
             send(
                 z_send.at[i], z_recv.at[i, k], z_send_sem.at[i, k], z_recv_sem.at[i, k],
                 (lax.rem(mz + dz, NZ), mx, my, mc),
             )
+
+    def column_sum(i, part):
         for k in range(len(COLUMN)):
             receive(z_recv.at[i, k], z_send_sem.at[i, k], z_recv_sem.at[i, k])
             part = part + z_recv[i, k].astype(jnp.float32)
-        whole[i, mc, mx, my] = part.astype(jnp.bfloat16)
+        part = part.astype(jnp.bfloat16)
+        whole[i, mc, mx, my] = part
+        return part
+
+    def gather(i):
         piece = whole.at[i, mc, mx, my]
         for k, (dx, dy) in enumerate(PLANE):
             px, py = shifted(dx, dy)
@@ -216,6 +262,10 @@
             send(piece, piece, far_send_sem.at[i, k], far_recv_sem.at[i, k], (mz, px, py, other))
         last = len(PLANE)
         send(piece, piece, far_send_sem.at[i, last], far_recv_sem.at[i, last], (mz, mx, my, other))
+
+    outs = []
+
+    def gathered(i, p):
         for k, (dx, dy) in enumerate(PLANE):
             px, py = shifted(NX - dx, NY - dy)
             receive(whole.at[i, mc, px, py], own_send_sem.at[i, k], own_recv_sem.at[i, k])
@@ -224,12 +274,71 @@
         out = pltpu.make_async_copy(block.at[i], solved_ref.at[p], out_sem.at[i])
         out.start()
         outs.append(out)
-        if p > 0:
-            entry = jnp.clip(p - own_pivot - 1, 0, PIV - 2)
-            active = holds * (own_pivot < p).astype(jnp.int32)
-            factor = matmul_t(columns, left[entry])
-            factor = jnp.where(rank_ids < coupling_ranks_ref[0, entry] * active, factor, 0.0)
-            acc[...] = acc[...] - matmul(factor.astype(jnp.bfloat16), gain[entry])
+        return columns
+
+    scatter(0, 2)
+    loads[0].wait()
+    loads[1].wait()
+    make_gain(0)
+    spread_pair()
+    swap.start()
+    part = scattered(0)
+    send_column(0, part)
+    make_gain(1)
+    column_sum(0, part)
+    gather(0)
+    columns = gathered(0, 2)
+    entry = jnp.clip(2 - own_pivot - 1, 0, PIV - 2)
+    active = holds * (own_pivot < 2).astype(jnp.int32)
+    factor = matmul_t(columns, left[entry])
+    factor = jnp.where(rank_ids < coupling_ranks_ref[0, entry] * active, factor, 0.0)
+    acc[...] = acc[...] - matmul(factor.astype(jnp.bfloat16), gain[entry])
+
+    scatter(1, 1)
+    rest = jnp.where(owner_ref[0] == me, acc[...], 0.0).reshape(NX, GROUP, B)
+    for g in range(NY):
+        rest_send[:, g] = rest[:, :, g * COLS : (g + 1) * COLS]
+    for k, (dx, dy) in enumerate(PLANE):
+        px, py = shifted(dx, dy)
+        send(
+            rest_send.at[px, py], rest_recv.at[k], rest_send_sem.at[k], rest_recv_sem.at[k],
+            (mz, px, py, mc),
+        )
+    share_pair()
+    part = scattered(1)
+    send_column(1, part)
+    swap_in.wait_recv()
+    for load in loads[2:]:
+        load.wait()
+    apply_future(0, 2)
+    slice_1 = column_sum(1, part)
+
+    take_pair()
+    for x in range(NX):
+        f_send[x] = matmul_t(slice_1, pair[0, x])
+    for k, d in enumerate(RING):
+        send(
+            f_send, f_recv.at[k], f_send_sem.at[k], f_recv_sem.at[k],
+            (mz, mx, lax.rem(my + d, NY), mc),
+        )
+    gather(1)
+    part = rest_send[mx, my]
+    for k in range(len(PLANE)):
+        receive(rest_recv.at[k], rest_send_sem.at[k], rest_recv_sem.at[k])
+        part = part + rest_recv[k]
+    for k in range(len(RING)):
+        receive(f_recv.at[k], f_send_sem.at[k], f_recv_sem.at[k])
+    for x in range(NX):
+        factor = f_send[x]
+        for k in range(len(RING)):
+            factor = factor + f_recv[k, x]
+        part = part - matmul(factor.astype(jnp.bfloat16), pair[1, x])
+    send_column(2, part)
+    gathered(1, 1)
+    apply_future(1, 1)
+    column_sum(2, part)
+    gather(2)
+    gathered(2, 0)
     apply_future(PIV - 1, 0)
     out = pltpu.make_async_copy(future, future_out_ref, out_sem.at[PIV])
     out.start()
@@ -247,7 +356,7 @@
 ):
     smem = pl.BlockSpec(memory_space=pltpu.SMEM)
     hbm = pl.BlockSpec(memory_space=pl.ANY)
-    plane, column = len(PLANE), len(COLUMN)
+    plane, column, ring = len(PLANE), len(COLUMN), len(RING)
     dma = pltpu.SemaphoreType.DMA
     bf16, f32 = jnp.bfloat16, jnp.float32
     solved, future_out = pl.pallas_call(
@@ -269,23 +378,40 @@
             pltpu.VMEM((PIV - 1, R, B), bf16),
             pltpu.VMEM((PROBES, B), f32),
             pltpu.VMEM((PIV, PROBES, B), bf16),
-            pltpu.VMEM((PIV, NX, NY, GROUP, COLS), bf16),
-            pltpu.VMEM((PIV, plane, GROUP, COLS), bf16),
+            pltpu.VMEM((PIV - 1, NX, NY, GROUP, COLS), bf16),
+            pltpu.VMEM((PIV - 1, plane, GROUP, COLS), bf16),
             pltpu.VMEM((PIV, GROUP, COLS), bf16),
             pltpu.VMEM((PIV, column, GROUP, COLS), bf16),
             pltpu.VMEM((PIV, NC, NX, NY, GROUP, COLS), bf16),
+            pltpu.VMEM((NX, NY, RANKS, COLS), bf16),
+            pltpu.VMEM((plane, RANKS, COLS), bf16),
+            pltpu.VMEM((NC, NX, RANKS, COLS), bf16),
+            pltpu.VMEM((NX, NY, GROUP, COLS), f32),
+            pltpu.VMEM((plane, GROUP, COLS), f32),
+            pltpu.VMEM((NX, GROUP, RANKS), f32),
+            pltpu.VMEM((ring, NX, GROUP, RANKS), f32),
             dma((6,)),
             dma((B // BLOCK,)),
             dma((PIV + 1,)),
             dma((2,)),
-            dma((PIV, plane)),
-            dma((PIV, plane)),
+            dma((PIV - 1, plane)),
+            dma((PIV - 1, plane)),
             dma((PIV, column)),
             dma((PIV, column)),
             dma((PIV, plane)),
             dma((PIV, plane)),
             dma((PIV, plane + 1)),
             dma((PIV, plane + 1)),
+            dma((plane,)),
+            dma((plane,)),
+            dma((ring,)),
+            dma((ring,)),
+            dma((ring + 1,)),
+            dma((ring + 1,)),
+            dma((plane,)),
+            dma((plane,)),
+            dma((ring,)),
+            dma((ring,)),
         ],
         compiler_params=pltpu.CompilerParams(collective_id=0, has_side_effects=True),
     )(

time: 64.7 us -> 64.2 us (level)
  no operation moved by 1% of the time
where the time goes in v2:
time: 64.2 us; the launch traced here: 64.1 us
  Pallas kernels  60 us (93%)
  local copies, waits for them, and re-layouts  3.46 us (5%)
    pallas_call x1, Pallas kernels, local(): pl.pallas_call(kernel, out_shape=(jax.ShapeDtypeStruct((PIV, PROBES, B),...  60 us
    unnamed x2, local copies, waits for them, and re-layouts  3.46 us

profile of v2, /device:TPU:1, one launch (start us, length us, event | category | flops | bytes accessed | tf_op | source)
XLA Modules:
  0.0 64.1 jit_solution(4279168763317289994)
XLA Ops:
  0.6 60.0 %shard_map.113 = (bf16[3,32,1536]{2,1,0:T(8,128)(2,1)}, f32[2,64,768]{2,1,0:T(8,128)}) custom-call(s32[3]{0:T(128)} %owner_ref.1, s32[1,2]{1,0:T(1,128)} %coupling_ranks_ref.1, s32[2,3]{1,0:T(2,128)} %future_ranks_ref.1, f32[32,1536]{1,0:T(8,128)} %bitcast.15, bf16[1536,1536]{1,0:T(8,128)(2,1)} %bitcast.11, bf16[2,200,1536]{2,1,0:T(8,128)(2,1)} %bitcast.12, ...), custom_call_target="tpu_custom_call" | custom-call | tf_op jit(solution)/shard_map/pallas_call | solution.py:362
  60.6 1.7 %copy.14 = bf16[3,1536,32]{1,2,0:T(8,128)(2,1)} copy(bf16[3,1536,32]{1,2,0:T(8,128)(2,1)} %bitcast.14) | data formatting | bytes 589824
  62.3 1.8 %copy.15 = f32[2,64,768]{2,1,0:T(8,128)} copy(f32[2,64,768]{2,1,0:T(8,128)} %get-tuple-element.9) | data formatting | bytes 786432

commit v3 on v2

--- a/solution.py
+++ b/solution.py
@@ -43,11 +43,11 @@
     solved_ref, future_out_ref,
     inverse, rhs, left, right, future_left, future_right, future, gain, acc, block,
     rs_send, rs_recv, z_send, z_recv, whole,
-    pair_send, pair_recv, pair, rest_send, rest_recv, f_send, f_recv,
+    pair_send, pair_recv, pair_mid, pair_last, pair, rest_send, rest_recv, f_send, f_recv,
     load_sem, panel_sem, out_sem, swap_sem,
     rs_send_sem, rs_recv_sem, z_send_sem, z_recv_sem,
     own_send_sem, own_recv_sem, far_send_sem, far_recv_sem,
-    pair_send_sem, pair_recv_sem, near_send_sem, near_recv_sem, cross_send_sem, cross_recv_sem,
+    pair_send_sem, pair_recv_sem, mid_send_sem, mid_recv_sem, near_send_sem, near_recv_sem, cross_send_sem, cross_recv_sem,
     rest_send_sem, rest_recv_sem, f_send_sem, f_recv_sem,
 ):
     mz, mx, my, mc = (lax.axis_index(name) for name in (*TC, "pr"))
@@ -161,32 +161,55 @@
             below = pl.ds(c * BLOCK, B - c * BLOCK)
             gain[j, :, columns] = matmul(right[j, :, below], inverse[below, columns]).astype(jnp.bfloat16)
 
+    first, second = mx + mc * (my - mx), my + mc * (mx - my)
+
+    def along_first(d):
+        return mz, lax.rem(mx + d * other, NX), lax.rem(my + d * mc, NY), mc
+
+    def along_second(d):
+        return mz, lax.rem(mx + d * mc, NX), lax.rem(my + d * other, NY), mc
+
+    def make_pair():
+        limit = jnp.where(owner_ref[0] == me, coupling_ranks_ref[0, 0], 0)
+
+        def factor_slice(ref, x, y, count):
+            return ref[0, pl.ds(x * RANKS, count), pl.ds(y * COLS, COLS)].astype(jnp.float32)
+
+        for a in range(NX):
+            for b in range(NY):
+                row, col = min(RANKS, R - a * RANKS), min(RANKS, R - b * RANKS)
+                ids = lax.broadcasted_iota(jnp.int32, (RANKS, COLS), 0)
+                left_part = factor_slice(left, a, b, row)
+                right_part = factor_slice(gain, b, a, col)
+                if row < RANKS:
+                    left_part = jnp.concatenate([left_part, jnp.zeros((RANKS - row, COLS), jnp.float32)])
+                if col < RANKS:
+                    right_part = jnp.concatenate([right_part, jnp.zeros((RANKS - col, COLS), jnp.float32)])
+                value = jnp.where(mc == 0, left_part, right_part)
+                start = (a + mc * (b - a)) * RANKS
+                pair_send[a, b] = jnp.where(ids + start < limit, value, 0.0).astype(jnp.bfloat16)
+
     def spread_pair():
-        limit = jnp.where(owner_ref[0] == me, coupling_ranks_ref[0, 0], 0)
-        for x in range(NX):
-            count = min(RANKS, R - x * RANKS)
-            rows = pl.ds(x * RANKS, count)
-            ids = lax.broadcasted_iota(jnp.int32, (count, COLS), 0) + x * RANKS
-            for y in range(NY):
-                columns = pl.ds(y * COLS, COLS)
-                value = jnp.where(
-                    mc == 0, left[0, rows, columns].astype(jnp.float32), gain[0, rows, columns].astype(jnp.float32)
-                )
-                pair_send[x, y, pl.ds(0, count)] = jnp.where(ids < limit, value, 0.0).astype(jnp.bfloat16)
-                if count < RANKS:
-                    pair_send[x, y, pl.ds(count, RANKS - count)] = jnp.zeros((RANKS - count, COLS), jnp.bfloat16)
-        for k, (dx, dy) in enumerate(PLANE):
-            px, py = shifted(dx, dy)
-            send(
-                pair_send.at[px, py], pair_recv.at[k], pair_send_sem.at[k], pair_recv_sem.at[k],
-                (mz, px, py, mc),
-            )
+        for k, d in enumerate(RING):
+            to = lax.rem(first + d, NX)
+            send(pair_send.at[to], pair_recv.at[k], pair_send_sem.at[k], pair_recv_sem.at[k], along_first(d))
+
+    def spread_on():
+        for k in range(len(RING)):
+            receive(pair_recv.at[k], pair_send_sem.at[k], pair_recv_sem.at[k])
+        total = pair_send[first].astype(jnp.float32)
+        for k in range(len(RING)):
+            total = total + pair_recv[k].astype(jnp.float32)
+        pair_mid[...] = total.astype(jnp.bfloat16)
+        for k, d in enumerate(RING):
+            to = lax.rem(second + d, NY)
+            send(pair_mid.at[to], pair_last.at[k], mid_send_sem.at[k], mid_recv_sem.at[k], along_second(d))
 
     def share_pair():
-        total = pair_send[mx, my].astype(jnp.float32)
-        for k in range(len(PLANE)):
-            receive(pair_recv.at[k], pair_send_sem.at[k], pair_recv_sem.at[k])
-            total = total + pair_recv[k].astype(jnp.float32)
+        total = pair_mid[second].astype(jnp.float32)
+        for k in range(len(RING)):
+            receive(pair_last.at[k], mid_send_sem.at[k], mid_recv_sem.at[k])
+            total = total + pair_last[k].astype(jnp.float32)
         pair[mc, mx] = total.astype(jnp.bfloat16)
         piece = pair.at[mc, mx]
         for k, d in enumerate(RING):
@@ -257,6 +280,8 @@
         for k, (dx, dy) in enumerate(PLANE):
             px, py = shifted(dx, dy)
             send(piece, piece, own_send_sem.at[i, k], own_recv_sem.at[i, k], (mz, px, py, mc))
+    def gather_far(i):
+        piece = whole.at[i, mc, mx, my]
         for k, (dx, dy) in enumerate(PLANE):
             px, py = shifted(dx, dy)
             send(piece, piece, far_send_sem.at[i, k], far_recv_sem.at[i, k], (mz, px, py, other))
@@ -280,6 +305,7 @@
     loads[0].wait()
     loads[1].wait()
     make_gain(0)
+    make_pair()
     spread_pair()
     swap.start()
     part = scattered(0)
@@ -287,6 +313,7 @@
     make_gain(1)
     column_sum(0, part)
     gather(0)
+    spread_on()
     columns = gathered(0, 2)
     entry = jnp.clip(2 - own_pivot - 1, 0, PIV - 2)
     active = holds * (own_pivot < 2).astype(jnp.int32)
@@ -307,10 +334,10 @@
     share_pair()
     part = scattered(1)
     send_column(1, part)
+    gather_far(0)
     swap_in.wait_recv()
     for load in loads[2:]:
         load.wait()
-    apply_future(0, 2)
     slice_1 = column_sum(1, part)
 
     take_pair()
@@ -322,6 +349,7 @@
             (mz, mx, lax.rem(my + d, NY), mc),
         )
     gather(1)
+    gather_far(1)
     part = rest_send[mx, my]
     for k in range(len(PLANE)):
         receive(rest_recv.at[k], rest_send_sem.at[k], rest_recv_sem.at[k])
@@ -335,9 +363,11 @@
         part = part - matmul(factor.astype(jnp.bfloat16), pair[1, x])
     send_column(2, part)
     gathered(1, 1)
+    apply_future(0, 2)
     apply_future(1, 1)
     column_sum(2, part)
     gather(2)
+    gather_far(2)
     gathered(2, 0)
     apply_future(PIV - 1, 0)
     out = pltpu.make_async_copy(future, future_out_ref, out_sem.at[PIV])
@@ -384,7 +414,9 @@
             pltpu.VMEM((PIV, column, GROUP, COLS), bf16),
             pltpu.VMEM((PIV, NC, NX, NY, GROUP, COLS), bf16),
             pltpu.VMEM((NX, NY, RANKS, COLS), bf16),
-            pltpu.VMEM((plane, RANKS, COLS), bf16),
+            pltpu.VMEM((ring, NY, RANKS, COLS), bf16),
+            pltpu.VMEM((NY, RANKS, COLS), bf16),
+            pltpu.VMEM((ring, RANKS, COLS), bf16),
             pltpu.VMEM((NC, NX, RANKS, COLS), bf16),
             pltpu.VMEM((NX, NY, GROUP, COLS), f32),
             pltpu.VMEM((plane, GROUP, COLS), f32),
@@ -402,8 +434,10 @@
             dma((PIV, plane)),
             dma((PIV, plane + 1)),
             dma((PIV, plane + 1)),
-            dma((plane,)),
-            dma((plane,)),
+            dma((ring,)),
+            dma((ring,)),
+            dma((ring,)),
+            dma((ring,)),
             dma((ring,)),
             dma((ring,)),
             dma((ring + 1,)),

time: 64.2 us -> 59 us (0.919)
  Pallas kernels: 60 us -> 54.8 us
    pallas_call x1, Pallas kernels: 60 us -> 54.8 us  [local(): pl.pallas_call(kernel, out_shape=(jax.ShapeDtypeStruct((PIV, PROBES, B),...]
where the time goes in v3:
time: 59 us; the launch traced here: 58.9 us
  Pallas kernels  54.8 us (93%)
  local copies, waits for them, and re-layouts  3.46 us (6%)
  between operations  0.64 us (1%)
    pallas_call x1, Pallas kernels, local(): pl.pallas_call(kernel, out_shape=(jax.ShapeDtypeStruct((PIV, PROBES, B),...  54.8 us
    unnamed x2, local copies, waits for them, and re-layouts  3.46 us

profile of v3, /device:TPU:1, one launch (start us, length us, event | category | flops | bytes accessed | tf_op | source)
XLA Modules:
  0.0 58.9 jit_solution(4054259612216928391)
XLA Ops:
  0.6 54.8 %shard_map.113 = (bf16[3,32,1536]{2,1,0:T(8,128)(2,1)}, f32[2,64,768]{2,1,0:T(8,128)}) custom-call(s32[3]{0:T(128)} %owner_ref.1, s32[1,2]{1,0:T(1,128)} %coupling_ranks_ref.1, s32[2,3]{1,0:T(2,128)} %future_ranks_ref.1, f32[32,1536]{1,0:T(8,128)} %bitcast.15, bf16[1536,1536]{1,0:T(8,128)(2,1)} %bitcast.11, bf16[2,200,1536]{2,1,0:T(8,128)(2,1)} %bitcast.12, ...), custom_call_target="tpu_custom_call" | custom-call | tf_op jit(solution)/shard_map/pallas_call | solution.py:392
  55.4 1.7 %copy.14 = bf16[3,1536,32]{1,2,0:T(8,128)(2,1)} copy(bf16[3,1536,32]{1,2,0:T(8,128)(2,1)} %bitcast.14) | data formatting | bytes 589824
  57.1 1.8 %copy.15 = f32[2,64,768]{2,1,0:T(8,128)} copy(f32[2,64,768]{2,1,0:T(8,128)} %get-tuple-element.9) | data formatting | bytes 786432

commit v4 on v3

--- a/solution.py
+++ b/solution.py
@@ -227,19 +227,30 @@
         last = len(RING)
         receive(pair.at[other, mx], cross_send_sem.at[last], cross_recv_sem.at[last])
 
-    def apply_future(i, p):
+    def take_far(i):
         for k, (dx, dy) in enumerate(PLANE):
             px, py = shifted(NX - dx, NY - dy)
             receive(whole.at[i, other, px, py], far_send_sem.at[i, k], far_recv_sem.at[i, k])
         receive(whole.at[i, other, mx, my], far_send_sem.at[i, len(PLANE)], far_recv_sem.at[i, len(PLANE)])
+
+    half = B // NC
+
+    def weighted(probes, f, p, ids):
+        weights = matmul_t(probes[:, :half], future_left[0, f, p]) + matmul_t(
+            probes[:, half:], future_left[1, f, p]
+        )
+        weights = jnp.where(ids < future_ranks_ref[f, p], weights, 0.0)
+        return matmul(weights.astype(jnp.bfloat16), future_right[f, p])
+
+    def apply_future(i, p):
+        take_far(i)
         both = jnp.concatenate([assembled(i, 0), assembled(i, 1)], axis=0)
-        half = B // NC
         for f in range(2):
-            weights = matmul_t(both[:, :half], future_left[0, f, p]) + matmul_t(
-                both[:, half:], future_left[1, f, p]
-            )
-            weights = jnp.where(future_rank_ids < future_ranks_ref[f, p], weights, 0.0)
-            future[f] = future[f] - matmul(weights.astype(jnp.bfloat16), future_right[f, p])
+            future[f] = future[f] - weighted(both, f, p, future_rank_ids)
+
+    def apply_future_half(p, core, probes, f):
+        rows = pl.ds(pl.multiple_of(core * PROBES, PROBES), PROBES)
+        future[f, rows] = future[f, rows] - weighted(probes, f, p, rank_ids)
 
     def scatter(i, p):
         masked = jnp.where(owner_ref[p] == me, acc[...], 0.0).reshape(NX, GROUP, B).astype(jnp.bfloat16)
@@ -368,16 +379,39 @@
     column_sum(2, part)
     gather(2)
     gather_far(2)
-    gathered(2, 0)
-    apply_future(PIV - 1, 0)
-    out = pltpu.make_async_copy(future, future_out_ref, out_sem.at[PIV])
-    out.start()
-    outs.append(out)
+    columns = gathered(2, 0)
+
+    def store(f):
+        out = pltpu.make_async_copy(future.at[f], future_out_ref.at[f], out_sem.at[PIV + f])
+        out.start()
+        outs.append(out)
+
+    for f in range(2):
+        apply_future_half(0, mc, columns, f)
+    take_far(PIV - 1)
+    columns = assembled(PIV - 1, other)
+    for f in range(2):
+        apply_future_half(0, other, columns, f)
+        store(f)
     for copy in sent:
         copy.wait_send()
     swap.wait_send()
     for out in outs:
         out.wait()
+
+
+def deliver(solved_ref, future_ref, solved_out_ref, future_out_ref, solved, future, in_sem, out_sem):
+    pairs = [(solved_ref.at[p], solved.at[p], solved_out_ref.at[p]) for p in range(PIV)]
+    pairs += [(future_ref.at[f], future.at[f], future_out_ref.at[f]) for f in range(2)]
+    arrivals = [pltpu.make_async_copy(a, b, in_sem.at[k]) for k, (a, b, _) in enumerate(pairs)]
+    leavings = [pltpu.make_async_copy(b, c, out_sem.at[k]) for k, (_, b, c) in enumerate(pairs)]
+    for arrival in arrivals:
+        arrival.start()
+    for arrival, leaving in zip(arrivals, leavings, strict=True):
+        arrival.wait()
+        leaving.start()
+    for leaving in leavings:
+        leaving.wait()
 
 
 def local(
@@ -424,7 +458,7 @@
             pltpu.VMEM((ring, NX, GROUP, RANKS), f32),
             dma((6,)),
             dma((B // BLOCK,)),
-            dma((PIV + 1,)),
+            dma((PIV + 2,)),
             dma((2,)),
             dma((PIV - 1, plane)),
             dma((PIV - 1, plane)),
@@ -460,6 +494,21 @@
         future_right,
         future_rhs,
     )
+    solved, future_out = pl.pallas_call(
+        deliver,
+        out_shape=(
+            jax.ShapeDtypeStruct(solved.shape, bf16),
+            jax.ShapeDtypeStruct(future_out.shape, f32),
+        ),
+        in_specs=[hbm, hbm],
+        out_specs=(hbm, hbm),
+        scratch_shapes=[
+            pltpu.VMEM(solved.shape, bf16),
+            pltpu.VMEM(future_out.shape, f32),
+            dma((PIV + 2,)),
+            dma((PIV + 2,)),
+        ],
+    )(solved, future_out)
     return solved.swapaxes(1, 2), future_out
 
 

time: 59 us -> 57.5 us (0.975)
  local copies, waits for them, and re-layouts: 3.46 us -> 0 us
  Pallas kernels: 54.8 us -> 56.7 us
    unnamed x2 -> x0, local copies, waits for them, and re-layouts: 3.46 us -> none
    pallas_call x0 -> x1, Pallas kernels: none -> 1.93 us  [local(): pl.pallas_call(deliver, out_shape=(jax.ShapeDtypeStruct(solved.shape, bf1...]
where the time goes in v4:
time: 57.5 us; the launch traced here: 57.4 us
  Pallas kernels  56.7 us (99%)
  between operations  0.64 us (1%)
    pallas_call x1, Pallas kernels, local(): pl.pallas_call(kernel, out_shape=(jax.ShapeDtypeStruct((PIV, PROBES, B),...  54.8 us
    pallas_call x1, Pallas kernels, local(): pl.pallas_call(deliver, out_shape=(jax.ShapeDtypeStruct(solved.shape, bf1...  1.93 us

profile of v4, /device:TPU:1, one launch (start us, length us, event | category | flops | bytes accessed | tf_op | source)
XLA Modules:
  0.0 57.4 jit_solution(13265077892193795349)
XLA Ops:
  0.6 54.8 %shard_map.113 = (bf16[3,32,1536]{2,1,0:T(8,128)(2,1)}, f32[2,64,768]{2,1,0:T(8,128)}) custom-call(s32[3]{0:T(128)} %owner_ref.1, s32[1,2]{1,0:T(1,128)} %coupling_ranks_ref.1, s32[2,3]{1,0:T(2,128)} %future_ranks_ref.1, f32[32,1536]{1,0:T(8,128)} %bitcast.14, bf16[1536,1536]{1,0:T(8,128)(2,1)} %bitcast.11, bf16[2,200,1536]{2,1,0:T(8,128)(2,1)} %bitcast.12, ...), custom_call_target="tpu_custom_call" | custom-call | tf_op jit(solution)/shard_map/pallas_call | solution.py:426
  55.4 1.9 %shard_map.114 = (bf16[3,32,1536]{2,1,0:T(8,128)(2,1)}, f32[2,64,768]{2,1,0:T(8,128)}) custom-call(bf16[3,32,1536]{2,1,0:T(8,128)(2,1)} %get-tuple-element.6.solved_ref, f32[2,64,768]{2,1,0:T(8,128)} %get-tuple-element.7.future_ref), custom_call_target="tpu_custom_call" | custom-call | tf_op jit(solution)/shard_map/pallas_call | solution.py:497

commit v5 on v4

--- a/solution.py
+++ b/solution.py
@@ -38,12 +38,13 @@
 
 
 def kernel(
-    owner_ref, coupling_ranks_ref, future_ranks_ref,
+    owner_in, coupling_ranks_in, future_ranks_in,
     rhs_ref, inverse_ref, left_ref, right_ref, future_left_ref, future_right_ref, future_rhs_ref,
     solved_ref, future_out_ref,
     inverse, rhs, left, right, future_left, future_right, future, gain, acc, block,
     rs_send, rs_recv, z_send, z_recv, whole,
     pair_send, pair_recv, pair_mid, pair_last, pair, rest_send, rest_recv, f_send, f_recv,
+    owner_ref, coupling_ranks_ref, future_ranks_ref, table_sem,
     load_sem, panel_sem, out_sem, swap_sem,
     rs_send_sem, rs_recv_sem, z_send_sem, z_recv_sem,
     own_send_sem, own_recv_sem, far_send_sem, far_recv_sem,
@@ -56,17 +57,6 @@
 
     def shifted(dx, dy):
         return lax.rem(mx + dx, NX), lax.rem(my + dy, NY)
-
-    rhs_load = pltpu.make_async_copy(rhs_ref, rhs, load_sem.at[0])
-    rhs_load.start()
-    panels = []
-    for k in range(B // BLOCK):
-        rows, columns = pl.ds(k * BLOCK, BLOCK), pl.ds(0, (k + 1) * BLOCK)
-        panel = pltpu.make_async_copy(
-            inverse_ref.at[rows, columns], inverse.at[rows, columns], panel_sem.at[k]
-        )
-        panel.start()
-        panels.append(panel)
 
     barrier = pltpu.get_barrier_semaphore()
     greeted = 0
@@ -81,6 +71,25 @@
         greeted += 1
     pl.semaphore_signal(barrier, 1, device_id=(mz, mx, my, other), device_id_type=MESH)
     greeted += 1
+
+    rhs_load = pltpu.make_async_copy(rhs_ref, rhs, load_sem.at[0])
+    rhs_load.start()
+    panels = []
+    for k in range(B // BLOCK):
+        rows, columns = pl.ds(k * BLOCK, BLOCK), pl.ds(0, (k + 1) * BLOCK)
+        panel = pltpu.make_async_copy(
+            inverse_ref.at[rows, columns], inverse.at[rows, columns], panel_sem.at[k]
+        )
+        panel.start()
+        panels.append(panel)
+
+    tables = [
+        pltpu.make_async_copy(owner_in, owner_ref, table_sem.at[0]),
+        pltpu.make_async_copy(coupling_ranks_in, coupling_ranks_ref, table_sem.at[1]),
+        pltpu.make_async_copy(future_ranks_in, future_ranks_ref, table_sem.at[2]),
+    ]
+    for table in tables:
+        table.start()
 
     loads = [
         pltpu.make_async_copy(right_ref, right, load_sem.at[1]),
@@ -124,6 +133,8 @@
         device_id_type=MESH,
     )
 
+    for table in tables:
+        table.wait()
     own_pivot = jnp.int32(0)
     holds = jnp.int32(0)
     for p in range(PIV):
@@ -295,6 +306,15 @@
         piece = whole.at[i, mc, mx, my]
         for k, (dx, dy) in enumerate(PLANE):
             px, py = shifted(dx, dy)
+            send(piece, piece, far_send_sem.at[i, k], far_recv_sem.at[i, k], (mz, px, py, other))
+        last = len(PLANE)
+        send(piece, piece, far_send_sem.at[i, last], far_recv_sem.at[i, last], (mz, mx, my, other))
+
+    def gather_both(i):
+        piece = whole.at[i, mc, mx, my]
+        for k, (dx, dy) in enumerate(PLANE):
+            px, py = shifted(dx, dy)
+            send(piece, piece, own_send_sem.at[i, k], own_recv_sem.at[i, k], (mz, px, py, mc))
             send(piece, piece, far_send_sem.at[i, k], far_recv_sem.at[i, k], (mz, px, py, other))
         last = len(PLANE)
         send(piece, piece, far_send_sem.at[i, last], far_recv_sem.at[i, last], (mz, mx, my, other))
@@ -377,8 +397,7 @@
     apply_future(0, 2)
     apply_future(1, 1)
     column_sum(2, part)
-    gather(2)
-    gather_far(2)
+    gather_both(2)
     columns = gathered(2, 0)
 
     def store(f):
@@ -418,7 +437,6 @@
     pivot_rhs, pivot_inverse, pivot_owner, coupling_left, coupling_right, coupling_ranks,
     future_left, future_right, future_ranks, future_rhs,
 ):
-    smem = pl.BlockSpec(memory_space=pltpu.SMEM)
     hbm = pl.BlockSpec(memory_space=pl.ANY)
     plane, column, ring = len(PLANE), len(COLUMN), len(RING)
     dma = pltpu.SemaphoreType.DMA
@@ -429,7 +447,7 @@
             jax.ShapeDtypeStruct((PIV, PROBES, B), bf16),
             jax.ShapeDtypeStruct(future_rhs.shape, f32),
         ),
-        in_specs=[smem] * 3 + [hbm] * 7,
+        in_specs=[hbm] * 10,
         out_specs=(hbm, hbm),
         scratch_shapes=[
             pltpu.VMEM((B, B), bf16),
@@ -456,6 +474,10 @@
             pltpu.VMEM((plane, GROUP, COLS), f32),
             pltpu.VMEM((NX, GROUP, RANKS), f32),
             pltpu.VMEM((ring, NX, GROUP, RANKS), f32),
+            pltpu.SMEM(pivot_owner.shape, jnp.int32),
+            pltpu.SMEM(coupling_ranks.shape, jnp.int32),
+            pltpu.SMEM(future_ranks.shape, jnp.int32),
+            dma((3,)),
             dma((6,)),
             dma((B // BLOCK,)),
             dma((PIV + 2,)),

time: 57.5 us -> 56.7 us (0.986)
  Pallas kernels: 56.7 us -> 55.9 us
    pallas_call x1, Pallas kernels: 54.8 us -> 54 us  [local(): pl.pallas_call(kernel, out_shape=(jax.ShapeDtypeStruct((PIV, PROBES, B),...]
where the time goes in v5:
time: 56.7 us; the launch traced here: 56.6 us
  Pallas kernels  55.9 us (99%)
  between operations  0.64 us (1%)
    pallas_call x1, Pallas kernels, local(): pl.pallas_call(kernel, out_shape=(jax.ShapeDtypeStruct((PIV, PROBES, B),...  54 us
    pallas_call x1, Pallas kernels, local(): pl.pallas_call(deliver, out_shape=(jax.ShapeDtypeStruct(solved.shape, bf1...  1.93 us

profile of v5, /device:TPU:1, one launch (start us, length us, event | category | flops | bytes accessed | tf_op | source)
XLA Modules:
  0.0 56.6 jit_solution(10628331057507901377)
XLA Ops:
  0.6 54.0 %shard_map.113 = (bf16[3,32,1536]{2,1,0:T(8,128)(2,1)}, f32[2,64,768]{2,1,0:T(8,128)}) custom-call(s32[3]{0:T(128)} %owner_in.1, s32[1,2]{1,0:T(1,128)} %coupling_ranks_in.1, s32[2,3]{1,0:T(2,128)} %future_ranks_in.1, f32[32,1536]{1,0:T(8,128)} %bitcast.14, bf16[1536,1536]{1,0:T(8,128)(2,1)} %bitcast.11, bf16[2,200,1536]{2,1,0:T(8,128)(2,1)} %bitcast.12, ...), custom_call_target="tpu_custom_call" | custom-call | tf_op jit(solution)/shard_map/pallas_call | solution.py:444
  54.6 1.9 %shard_map.114 = (bf16[3,32,1536]{2,1,0:T(8,128)(2,1)}, f32[2,64,768]{2,1,0:T(8,128)}) custom-call(bf16[3,32,1536]{2,1,0:T(8,128)(2,1)} %get-tuple-element.6.solved_ref, f32[2,64,768]{2,1,0:T(8,128)} %get-tuple-element.7.future_ref), custom_call_target="tpu_custom_call" | custom-call | tf_op jit(solution)/shard_map/pallas_call | solution.py:519

commit v6 on v5

--- a/solution.py
+++ b/solution.py
@@ -60,15 +60,15 @@
 
     barrier = pltpu.get_barrier_semaphore()
     greeted = 0
+    for dz in COLUMN:
+        pz = lax.rem(mz + dz, NZ)
+        pl.semaphore_signal(barrier, 1, device_id=(pz, mx, my, mc), device_id_type=MESH)
+        greeted += 1
     for dx, dy in PLANE:
         px, py = shifted(dx, dy)
         for core in (mc, other):
             pl.semaphore_signal(barrier, 1, device_id=(mz, px, py, core), device_id_type=MESH)
             greeted += 1
-    for dz in COLUMN:
-        pz = lax.rem(mz + dz, NZ)
-        pl.semaphore_signal(barrier, 1, device_id=(pz, mx, my, mc), device_id_type=MESH)
-        greeted += 1
     pl.semaphore_signal(barrier, 1, device_id=(mz, mx, my, other), device_id_type=MESH)
     greeted += 1
 
@@ -353,6 +353,9 @@
     acc[...] = acc[...] - matmul(factor.astype(jnp.bfloat16), gain[entry])
 
     scatter(1, 1)
+    share_pair()
+    part = scattered(1)
+    send_column(1, part)
     rest = jnp.where(owner_ref[0] == me, acc[...], 0.0).reshape(NX, GROUP, B)
     for g in range(NY):
         rest_send[:, g] = rest[:, :, g * COLS : (g + 1) * COLS]
@@ -362,9 +365,6 @@
             rest_send.at[px, py], rest_recv.at[k], rest_send_sem.at[k], rest_recv_sem.at[k],
             (mz, px, py, mc),
         )
-    share_pair()
-    part = scattered(1)
-    send_column(1, part)
     gather_far(0)
     swap_in.wait_recv()
     for load in loads[2:]:

time: 56.7 us -> 56.4 us (level)
  no operation moved by 1% of the time
where the time goes in v6:
time: 56.4 us; the launch traced here: 56.3 us
  Pallas kernels  55.6 us (99%)
  between operations  0.64 us (1%)
    pallas_call x1, Pallas kernels, local(): pl.pallas_call(kernel, out_shape=(jax.ShapeDtypeStruct((PIV, PROBES, B),...  53.7 us
    pallas_call x1, Pallas kernels, local(): pl.pallas_call(deliver, out_shape=(jax.ShapeDtypeStruct(solved.shape, bf1...  1.93 us

profile of v6, /device:TPU:1, one launch (start us, length us, event | category | flops | bytes accessed | tf_op | source)
XLA Modules:
  0.0 56.3 jit_solution(13826632251463776046)
XLA Ops:
  0.6 53.7 %shard_map.113 = (bf16[3,32,1536]{2,1,0:T(8,128)(2,1)}, f32[2,64,768]{2,1,0:T(8,128)}) custom-call(s32[3]{0:T(128)} %owner_in.1, s32[1,2]{1,0:T(1,128)} %coupling_ranks_in.1, s32[2,3]{1,0:T(2,128)} %future_ranks_in.1, f32[32,1536]{1,0:T(8,128)} %bitcast.14, bf16[1536,1536]{1,0:T(8,128)(2,1)} %bitcast.11, bf16[2,200,1536]{2,1,0:T(8,128)(2,1)} %bitcast.12, ...), custom_call_target="tpu_custom_call" | custom-call | tf_op jit(solution)/shard_map/pallas_call | solution.py:444
  54.4 1.9 %shard_map.114 = (bf16[3,32,1536]{2,1,0:T(8,128)(2,1)}, f32[2,64,768]{2,1,0:T(8,128)}) custom-call(bf16[3,32,1536]{2,1,0:T(8,128)(2,1)} %get-tuple-element.6.solved_ref, f32[2,64,768]{2,1,0:T(8,128)} %get-tuple-element.7.future_ref), custom_call_target="tpu_custom_call" | custom-call | tf_op jit(solution)/shard_map/pallas_call | solution.py:519
